TPU v7x, 256 devices: a whole 4x4x8 slice. The times are simulated.
256 devices in a mesh: sec: 8 (over x, core), term: 32 (over y, z).
Axes of the slice: x: 4, y: 4, z: 8, core: 2. Of those that a mesh axis runs over, the one named last changes fastest.
Arguments:
- env_blocks: bfloat16 [32, 16, 256, 256], P('term', 'sec'), may hold values from -6 to 6
- core_blocks: bfloat16 [512, 256, 256], P('sec', 'term'), may hold values from -0.375 to 0.375
- mpo_coeffs: bfloat16 [32, 32, 512], P(None, None, 'sec'), may hold values from -1 to 1
- pair_left: int32 [512], P('sec'), may hold values from 0 to 1
- pair_right: int32 [512], P('sec'), may hold values from 0 to 15
- block_dims: int32 [16], replicated, may hold values from 1 to 256, 3072 in all
Outputs:
- new_env: float32 [32, 16, 256, 256], P('term', 'sec')
Inputs may be any that keep to these rules, and one draw needn't show every extreme that they name: `pair_left`: A pair's left block is one of the 2 blocks of the sec index that holds the pair.
All inputs are finite; a program needn't handle non-finite values.
Results may differ from a plain program's by a relative error of at most 0.004.
Values may be sent and summed in bfloat16 or wider, within the bound.
A program may use at most 128 MiB of HBM per device.

v0:
```python
import jax
import jax.numpy as jnp
from jax import lax
from jax.sharding import PartitionSpec as P


def split_up(array, dim, peers):
    before, after = (array.shape[:dim], array.shape[dim + 1 :])
    return jnp.moveaxis(array.reshape(*before, peers, -1, *after), dim, 0)


def sum_at_owner(array, axis, dim):
    peers = lax.axis_size(axis)
    pieces = lax.all_to_all(split_up(array, dim, peers), axis, 0, 0, tiled=True)
    return jnp.sum(pieces, axis=0)


def per_device(env_blocks, core_blocks, mpo_coeffs, pair_left, pair_right, block_dims):
    nb_local = env_blocks.shape[1]
    blk = env_blocks.shape[2]
    pairs_local = core_blocks.shape[0]
    total_blocks = block_dims.shape[0]
    sec_index = lax.axis_index("sec")
    term_index = lax.axis_index("term")
    core_full = lax.all_gather(core_blocks, "term", axis=1, tiled=True)
    block_ids = jnp.arange(total_blocks)
    left_global = sec_index * nb_local + pair_left
    dims_left = jnp.sum(
        jnp.where(left_global[:, None] == block_ids[None, :], block_dims[None, :], 0), axis=1
    )
    right_match = pair_right[:, None] == block_ids[None, :]
    dims_right = jnp.sum(jnp.where(right_match, block_dims[None, :], 0), axis=1)
    rows = jnp.arange(blk)
    keep = (rows[None, :, None] < dims_left[:, None, None]) & (
        rows[None, None, :] < dims_right[:, None, None]
    )
    masked = jnp.where(keep, core_full, jnp.zeros((), core_full.dtype))
    left_onehot = (pair_left[:, None] == jnp.arange(nb_local)[None, :]).astype(jnp.bfloat16)
    own_coeffs = lax.dynamic_index_in_dim(mpo_coeffs, term_index, 1, keepdims=False)
    piece = lax.all_gather(env_blocks, "term", axis=0, tiled=True)
    count = piece.shape[0]
    weights = own_coeffs[:, :, None] * left_onehot[None, :, :]
    flat = piece.reshape(count, nb_local, blk * blk)
    summed_terms = jnp.einsum("wpi,wix->px", weights, flat, preferred_element_type=jnp.float32)
    mixed = summed_terms.astype(jnp.bfloat16).reshape(pairs_local, blk, blk)
    half = jnp.einsum("prc,pcd->prd", mixed, masked, preferred_element_type=jnp.float32).astype(
        jnp.bfloat16
    )
    pair_terms = jnp.einsum("prc,prd->pcd", masked, half, preferred_element_type=jnp.float32)
    pair_terms = pair_terms.reshape(pairs_local, blk * blk)
    right_onehot = right_match.astype(jnp.float32)
    owned = sum_at_owner(
        jnp.dot(
            right_onehot.T,
            pair_terms,
            precision=lax.Precision.HIGHEST,
            preferred_element_type=jnp.float32,
        ),
        "sec",
        0,
    )
    return owned.reshape(1, nb_local, blk, blk)


def solution(mesh):
    return jax.shard_map(
        per_device,
        mesh=mesh,
        in_specs=(
            P("term", "sec", None, None),
            P("sec", "term", None),
            P(None, None, "sec"),
            P("sec"),
            P("sec"),
            P(),
        ),
        out_specs=P("term", "sec", None, None),
        check_vma=False,
    )
```

profile of v0, /device:TPU:1, one launch (start us, length us, event | category | flops | bytes accessed | tf_op | source)
XLA Modules:
  0.0 324.6 jit_solution(13647272893543834493)
XLA Ops:
  6.5 0.0 copy-start
  6.5 0.0 all-gather.5.cloned.1.call-start
  6.5 0.7 all-gather.5.cloned.1.call-update
  7.3 0.0 all-gather.3.cloned.1.call-start
  7.3 0.7 all-gather.3.cloned.1.call-update
  8.0 0.0 copy-done
  8.1 0.7 broadcast_add_fusion
  8.7 0.8 select_reduce_fusion.1
  9.5 0.7 compare_convert_fusion
  10.2 0.1 iota_compare_fusion
  10.3 100.6 %all-gather.5.cloned.1.call-done = bf16[32,2,256,256]{3,2,1,0:T(8,128)(2,1)} async-done(((bf16[1,2,256,256]{3,2,1,0:T(8,128)(2,1)}), bf16[32,2,256,256]{3,2,1,0:T(8,128)(2,1)}) %all-gather.5.cloned.1.call-update) | async-done | bytes 8388624 | tf_op jit(solution)/shard_map/all_gather | solution.py:40
  110.9 19.8 %reshape.106 = bf16[32,2,65536]{2,1,0:T(2,128)(2,1)} reshape(bf16[32,2,256,256]{3,2,1,0:T(8,128)(2,1)} %all-gather.5.cloned.1.call-done) | data formatting | bytes 16777216 | tf_op jit(solution)/shard_map/reshape | solution.py:43
  130.7 13.2 %fusion = bf16[64,65536]{1,0:T(8,128)(2,1)} fusion(bf16[32,2,65536]{2,1,0:T(2,128)(2,1)} %reshape.106, bf16[64,2]{0,1:T(2,128)(2,1)S(1)} %compare_convert_fusion, bf16[32,64]{1,0:T(8,128)(2,1)S(1)} %bitcast.26), kind=kOutput, calls=%fused_computation.1 | convolution fusion | flops 541069312 | bytes 16781568 | tf_op jit(solution)/shard_map/wpi,wix->px/dot_general | solution.py:44
  143.8 8.9 %copy.23 = bf16[8,8,256,256]{3,2,1,0:T(8,128)(2,1)} copy(bf16[8,8,256,256]{3,1,2,0:T(8,128)(2,1)} %bitcast.23) | data formatting | bytes 16777216
  152.7 57.5 %all-gather.3.cloned.1.call-done = bf16[64,256,256]{2,1,0:T(8,128)(2,1)} async-done(((bf16[64,8,256]{2,1,0:T(8,128)(2,1)}), bf16[64,256,256]{2,1,0:T(8,128)(2,1)}) %all-gather.3.cloned.1.call-update) | async-done | bytes 8388624 | tf_op jit(solution)/shard_map/all_gather | solution.py:25
  210.3 0.0 copy-start.2
  210.3 9.4 %fusion.30 = bf16[64,256,256]{2,1,0:T(8,128)(2,1)S(1)} fusion(bf16[64,256,256]{2,1,0:T(8,128)(2,1)} %bitcast.24, bf16[64,256,256]{2,1,0:T(8,128)(2,1)} %all-gather.3.cloned.1.call-done, pred[64,256]{1,0:T(8,128)(4,1)S(1)} %get-tuple-element.7, pred[64,256]{1,0:T(8,128)(4,1)S(1)} %get-tuple-element.8), kind=kOutput, calls=%fused_computation.5.clone.2 | convolution fusion | flops 2160066560 | bytes 25198592 | tf_op jit(solution)/shard_map/prc,pcd->prd/dot_general | solution.py:46
  219.6 0.0 copy-done.2
  219.6 9.8 %fusion.2 = f32[64,256,256]{2,1,0:T(8,128)} fusion(bf16[64,256,256]{2,1,0:T(8,128)(2,1)S(1)} %copy-done.2, pred[64,256]{1,0:T(8,128)(4,1)S(1)} %get-tuple-element.7, pred[64,256]{1,0:T(8,128)(4,1)S(1)} %get-tuple-element.8, bf16[64,256,256]{2,1,0:T(8,128)(2,1)S(1)} %fusion.30), kind=kOutput, calls=%fused_computation.4 | convolution fusion | flops 2155872256 | bytes 33587200 | tf_op jit(solution)/shard_map/prc,prd->pcd/dot_general | solution.py:49
  229.4 0.0 copy-start.3
  229.4 14.5 %reshape.105 = f32[64,65536,1]{1,0,2:T(8,128)} reshape(f32[64,256,256]{2,1,0:T(8,128)} %fusion.2) | data formatting | bytes 33554432 | tf_op jit(solution)/shard_map/reshape | solution.py:50
  243.9 0.0 copy-done.3
  243.9 9.3 %fusion.15 = f32[8,2,65536]{2,0,1:T(8,128)S(1)} fusion(f32[64,65536,1]{1,0,2:T(8,128)} %reshape.105, s32[8,2]{0,1:T(2,128)S(1)} %multiply_add_fusion, s32[64]{0:T(128)S(1)} %copy-done.3), kind=kOutput, calls=%fused_computation.21 | convolution fusion | flops 805307392 | bytes 20971840 | tf_op jit(solution)/shard_map/dot_general | solution.py:53
  253.3 0.0 copy-start.1
  253.3 3.2 copy.19
  256.6 56.7 %all_to_all.5 = f32[8,2,65536]{2,1,0:T(2,128)} all-to-all(f32[8,2,65536]{2,1,0:T(2,128)S(1)} %copy.19), channel_id=1, replica_groups=mesh['sec'=8,'term'=32] {'sec'}, dimensions={0} | all-to-all | bytes 8388608 | tf_op jit(solution)/shard_map/all_to_all | solution.py:14
  313.2 3.7 %reduce_sum.29 = f32[2,65536]{1,0:T(2,128)S(1)} reduce(f32[8,2,65536]{2,1,0:T(2,128)} %all_to_all.5, f32[]{:T(128)} %constant.22.clone.1), dimensions={0}, to_apply=%region_2.3 | reduce | flops 917504 | bytes 4718596 | tf_op jit(solution)/shard_map/reduce_sum | solution.py:15
  317.0 0.8 copy.29
  317.8 0.0 copy-done.1
  (3 shorter events, 0.0 us)
Async XLA Ops:
  6.5 1.5 copy-start
  6.5 104.3 %all-gather.5.cloned.1.call-start = ((), (), s32[]{:S(2)}) async-start(), calls=%async_computation.2 | async-start | bytes 8650752 | tf_op jit(solution)/shard_map/all_gather | solution.py:40
  7.3 203.0 %all-gather.3.cloned.1.call-start = ((), (), s32[]{:S(2)}) async-start(), calls=%async_computation.1 | async-start | bytes 8650752 | tf_op jit(solution)/shard_map/all_gather | solution.py:25
  210.3 9.4 %copy-start.2 = (bf16[64,256,256]{2,1,0:T(8,128)(2,1)S(1)}, bf16[64,256,256]{2,1,0:T(8,128)(2,1)}, u32[]{:S(2)}) copy-start(bf16[64,256,256]{2,1,0:T(8,128)(2,1)} %all-gather.3.cloned.1.call-done) | copy-start | bytes 25165828
  229.4 14.5 %copy-start.3 = (s32[64]{0:T(128)S(1)}, s32[64]{0:T(128)}, u32[]{:S(2)}) copy-start(s32[64]{0:T(128)} %param.10) | copy-start | bytes 772
  253.3 64.5 %copy-start.1 = (bf16[32,32,64]{2,1,0:T(8,128)(2,1)S(1)}, bf16[32,32,64]{2,1,0:T(8,128)(2,1)}, u32[]{:S(2)}) copy-start(bf16[32,32,64]{2,1,0:T(8,128)(2,1)} %param.8) | copy-start | bytes 393220
Sparse Core Ops, SparseCore 0:
  9.9 100.9 all-gather.4
  113.3 96.8 all-gather.2
where the time goes:
time: 326 us; the launch traced here: 325 us
  waiting for transfers between devices  160 us (49%)
  blocking collectives  56.7 us (17%)
  local copies, waits for them, and re-layouts  47.3 us (15%)
  matrix products  41.6 us (13%)
  between operations  13.5 us (4%)
  other arithmetic  5.9 us (2%)
    all_gather x1, waiting for transfers between devices, per_device(): piece = lax.all_gather(env_blocks, 'term', axis=0, tiled=True)  101 us
    all_gather x1, waiting for transfers between devices, per_device(): core_full = lax.all_gather(core_blocks, 'term', axis=1, tiled=True)  57.5 us
    all_to_all x1, blocking collectives, sum_at_owner(): pieces = lax.all_to_all(split_up(array, dim, peers), axis, 0, 0, tiled=True)  56.7 us
    reshape x1, local copies, waits for them, and re-layouts, per_device(): flat = piece.reshape(count, nb_local, blk * blk)  19.8 us
    reshape x1, local copies, waits for them, and re-layouts, per_device(): pair_terms = pair_terms.reshape(pairs_local, blk * blk)  14.5 us
    dot_general x1, matrix products, per_device(): jnp.einsum('wpi,wix->px', weights, flat, preferred_element_type=jnp.float32)  13.2 us
    dot_general x1, matrix products, per_device(): jnp.einsum('prc,prd->pcd', masked, half, preferred_element_type=jnp.float32)  9.76 us
    unnamed x11, local copies, waits for them, and re-layouts  9.72 us
  transfers between devices with their start and end apart: 2, of which 2 were waited for; matrix products, arithmetic and copies ran while one was open for 14% of the time, Pallas kernels for 0%

commit v1 on v0

v1 whole, which is shorter than its diff:
```python
import jax
import jax.numpy as jnp
from jax import lax
from jax.experimental import pallas as pl
from jax.experimental.pallas import tpu as pltpu
from jax.sharding import PartitionSpec as P

MESH = pl.DeviceIdType.MESH
PAIRS = 64
ROWS = 64
ENV = tuple(range(0, 256, ROWS))
CORE = ((0, 16), (16, 16), (32, 16), (48, 8), (56, 8))
STAGES = len(ENV) + len(CORE)
BLK = 256
F32, BF16 = jnp.float32, jnp.bfloat16


def rem(a, n):
    return lax.rem(a + n, n)


def kernel(
    env_in, core_in, w_in, meta_in, fin_f, fin_z,
    env_all, core_all, mixed, run, kron, wbuf, mbuf, mscal,
    obuf, r1, r2m, r2p, fin_s, zs,
    rs, ds, dss, ss, own, own_s, meta_r, meta_s, sc_sem,
    xr1, xrm, xrp, xs, fr, fd, fs,
):
    sec, term = lax.axis_index("sec"), lax.axis_index("term")
    x, c, y, z = sec // 2, lax.rem(sec, 2), term // 8, lax.rem(term, 8)
    par = lax.rem(z, 2)
    z1 = z + 1 - 2 * par
    other = 1 - c
    role = lax.rem(c + par, 2)
    zr = z + role * (1 - 2 * par)
    t_own, t_role = 8 * y + z, 8 * y + zr

    def dev(x_=None, y_=None, z_=None, c_=None):
        x_ = x if x_ is None else x_
        y_ = y if y_ is None else y_
        z_ = z if z_ is None else z_
        c_ = c if c_ is None else c_
        return {"sec": 2 * x_ + c_, "term": 8 * y_ + z_}

    partner = dev(c_=other)
    near = {
        ("z", 1): dev(z_=rem(z + 2, 8)), ("z", -1): dev(z_=rem(z - 2, 8)),
        ("y", 1): dev(y_=rem(y + 1, 4)), ("y", -1): dev(y_=rem(y - 1, 4)),
        ("x", 1): dev(x_=rem(x + 1, 4)), ("x", -1): dev(x_=rem(x - 1, 4)),
    }
    across = [dev(z_=z1, c_=0), dev(z_=z1, c_=1)]
    swap = dev(z_=z1, c_=other)

    barrier = pltpu.get_barrier_semaphore()
    greet = [partner, *near.values(), *across]
    for who in greet:
        pl.semaphore_signal(barrier, inc=1, device_id=who, device_id_type=MESH)
    pl.semaphore_wait(barrier, len(greet))

    def remote(src, dst, send, recv, who):
        return pltpu.make_async_remote_copy(
            src_ref=src, dst_ref=dst, send_sem=send, recv_sem=recv,
            device_id=who, device_id_type=MESH,
        )

    def shard(i, t, whole):
        if i < len(ENV):
            rows = pl.ds(ENV[i], ROWS)
            return whole[0].at[t, :, rows, :] if t is not None else whole[0].at[:, rows, :]
        some = pl.ds(*CORE[i - len(ENV)])
        if t is None:
            return whole[1].at[some]
        return whole[1].at[some, pl.ds(pl.multiple_of(8 * t, 8), 8), :]

    held, given = (env_all, core_all), (env_in, core_in)

    def place_own(stages):
        @pl.when(role == 0)
        def _():
            for i in stages:
                pltpu.make_async_copy(shard(i, None, given), shard(i, t_own, held), own.at[i]).start()

        @pl.when(role == 1)
        def _():
            for i in stages:
                remote(shard(i, None, given), shard(i, t_own, held), own_s.at[i], own.at[i], swap).start()

    DIMS = (("z", "y"), ("y", "z"))
    OFFS = (0, -1, 1, 2)

    def piece(i, color, half, off1, off2):
        dz, dy = (off1, off2) if color == 0 else (off2, off1)
        t = 8 * rem(y + dy, 4) + rem(zr + 2 * dz + 8, 8)
        first, count = (ENV[i], ROWS) if i < len(ENV) else CORE[i - len(ENV)]
        first, count = (first, 3 * count // 4) if color == 0 else (first + 3 * count // 4, count // 4)
        if i < len(ENV):
            rows = pl.ds(first, count)
            return env_all.at[t, :, rows, :] if half is None else env_all.at[t, half, rows, :]
        if half is not None:
            count //= 2
            first += half * count
        return core_all.at[pl.ds(first, count), pl.ds(pl.multiple_of(8 * t, 8), 8), :]

    def send(i, color, half, off1, off2, dim, sign, slot):
        ref = piece(i, color, half, off1, off2)
        remote(ref, ref, ss.at[i], rs.at[i, color, slot], near[dim, sign]).start()

    def take(i, color, half, off1, off2, slot):
        ref = piece(i, color, half, off1, off2)
        remote(ref, ref, ss.at[i], rs.at[i, color, slot], partner).wait_recv()

    def share(i, color, half, off1, off2):
        ref = piece(i, color, half, off1, off2)
        remote(ref, ref, dss.at[i], ds.at[i], partner).start()

    def start_own(i):
        pltpu.make_async_copy(shard(i, None, given), shard(i, t_role, held), own.at[i]).wait()
        for color, (d1, d2) in enumerate(DIMS):
            send(i, color, None, 0, 0, d1, 1, 0)
            send(i, color, None, 0, 0, d1, -1, 1)
            send(i, color, None, 0, 0, d2, 1, 4)
            send(i, color, None, 0, 0, d2, -1, 5)
        for color in range(2):
            share(i, color, None, 0, 0)

    def second(i, color, b):
        d2 = DIMS[color][1]
        send(i, color, None, OFFS[b], 0, d2, 1, 4 + 4 * b)
        send(i, color, None, OFFS[b], 0, d2, -1, 5 + 4 * b)

    def first_near(i):
        for color, (d1, _) in enumerate(DIMS):
            for side, (off, sign) in enumerate(((-1, 1), (1, -1))):
                take(i, color, None, off, 0, side)
                send(i, color, side, off, 0, d1, sign, 2 + side)
                second(i, color, 1 + side)
                share(i, color, None, off, 0)

    def first_far(i):
        for color in range(2):
            take(i, color, 0, 2, 0, 2)
            take(i, color, 1, 2, 0, 3)
            second(i, color, 3)
            share(i, color, None, 2, 0)

    def second_near(i, blocks):
        for b in blocks:
            for color, (_, d2) in enumerate(DIMS):
                for side, (off, sign) in enumerate(((-1, 1), (1, -1))):
                    take(i, color, None, OFFS[b], off, 4 + 4 * b + side)
                    send(i, color, side, OFFS[b], off, d2, sign, 6 + 4 * b + side)
                    share(i, color, None, OFFS[b], off)

    def second_far(i, blocks):
        for b in blocks:
            for color in range(2):
                take(i, color, 0, OFFS[b], 2, 6 + 4 * b)
                take(i, color, 1, OFFS[b], 2, 7 + 4 * b)
                share(i, color, None, OFFS[b], 2)

    def total(i, blocks):
        n = 8 if i < len(ENV) else CORE[i - len(ENV)][1] // 2
        return core_all.at[pl.ds(0, n), pl.ds(0, 16 * blocks), :]

    def partner_done(i):
        ref = total(i, 16)
        remote(ref, ref, dss.at[i], ds.at[i], partner).wait_recv()

    def sends_done(i):
        ref = total(i, 15)
        remote(ref, ref, ss.at[i], ds.at[i], partner).wait_send()
        ref = total(i, 16)
        remote(ref, ref, dss.at[i], ds.at[i], partner).wait_send()

    n8 = 8 * PAIRS

    def set_weights():
        up = (lax.broadcasted_iota(jnp.int32, (n8, PAIRS), 0) // 8
              == lax.broadcasted_iota(jnp.int32, (n8, PAIRS), 1)).astype(F32).astype(BF16)
        left = jnp.dot(up, wbuf[...], preferred_element_type=F32).astype(BF16)
        full = lax.dot_general(left, up, (((1,), (1,)), ((), ())), preferred_element_type=F32)
        same_row = (lax.rem(lax.broadcasted_iota(jnp.int32, (n8, n8), 0), 8)
                    == lax.rem(lax.broadcasted_iota(jnp.int32, (n8, n8), 1), 8))
        kron[...] = jnp.where(same_row, full, 0.0).astype(BF16)
        run[0] = jnp.zeros((BLK, BLK), F32)

    def mix(lo, count):
        def one(g, carry):
            rows = pl.ds(pl.multiple_of(lo + 16 * g, 16), 16)
            e = env_all[:, :, rows, :]
            parts = [
                jnp.dot(kron[...], e[:, :, 8 * h : 8 * h + 8].reshape(n8, BLK), preferred_element_type=F32)
                for h in range(2)
            ]
            both = jnp.concatenate([m.reshape(PAIRS, 8, BLK) for m in parts], axis=1)
            mixed[:, rows, :] = both.astype(BF16)
            return carry

        lax.fori_loop(0, count // 16, one, 0)

    def pairs(lo, count):
        def four(i, carry):
            for u in range(4):
                k = lo + 4 * i + u
                m = core_all[k]
                h = jnp.dot(mixed[k], m, preferred_element_type=F32).astype(BF16)
                t = lax.dot_general(m, h, (((0,), (0,)), ((), ())), preferred_element_type=F32)
                run[k + 1] = t + run[k] * mscal[0, k].astype(F32)
            return carry

        lax.fori_loop(0, count // 4, four, 0)

    def compute(i, half):
        if i < 0:
            return
        if i < len(ENV):
            mix(ENV[i] + half * (ROWS // 2), ROWS // 2)
        else:
            lo, count = CORE[i - len(ENV)]
            pairs(lo + half * (count // 2), count // 2)

    place_own(range(len(ENV)))

    @pl.when(role == 0)
    def _():
        pltpu.make_async_copy(w_in.at[0], wbuf, meta_r.at[0]).start()
        pltpu.make_async_copy(meta_in, mbuf, meta_r.at[1]).start()
        remote(w_in.at[1], wbuf, meta_s.at[0], meta_r.at[0], partner).start()
        remote(meta_in, mbuf, meta_s.at[1], meta_r.at[1], partner).start()

    start_own(0)
    start_own(1)
    place_own(range(len(ENV), STAGES))
    pltpu.make_async_copy(w_in.at[0], wbuf, meta_r.at[0]).wait()
    pltpu.make_async_copy(meta_in, mbuf, meta_r.at[1]).wait()
    to_scalar = pltpu.make_async_copy(mbuf, mscal, sc_sem)
    to_scalar.start()
    set_weights()
    to_scalar.wait()
    first_near(0)
    for i in range(STAGES + 2):
        if i + 2 < STAGES:
            start_own(i + 2)
        if i + 1 < STAGES:
            first_near(i + 1)
        if i < STAGES:
            second_near(i, (0,))
            first_far(i)
        if 1 <= i <= STAGES:
            second_far(i - 1, (0,))
            second_near(i - 1, (3,))
        compute(i - 3, 0)
        if i < STAGES:
            second_near(i, (1, 2))
        if 1 <= i <= STAGES:
            second_far(i - 1, (1, 2))
        if i >= 2:
            second_far(i - 2, (3,))
        compute(i - 3, 1)
        if i >= 2:
            partner_done(i - 2)
    compute(STAGES - 1, 0)
    compute(STAGES - 1, 1)

    def part(xj, q):
        return run[mscal[0, PAIRS + 4 * xj + q]]

    far, fwd, back = rem(x + 2, 4), rem(x + 1, 4), rem(x - 1, 4)

    def hop(n, q, dst, recv, sign):
        return remote(obuf.at[4 * n + q], dst.at[q], xs.at[4 * n + q], recv.at[q], near["x", sign])

    def to_far(q):
        obuf[q] = part(far, q).astype(BF16)
        hop(0, q, r1, xr1, 1 if q < 2 else -1).start()

    def to_next(q, sign, add):
        value = part(fwd if sign == 1 else back, q)
        n, dst, recv = (1, r2m, xrm) if sign == 1 else (2, r2p, xrp)
        if add:
            hop(0, q, r1, xr1, 1).wait_recv()
            value = value + r1[q].astype(F32)
        obuf[4 * n + q] = value.astype(BF16)
        hop(n, q, dst, recv, sign).start()

    for q in (0, 2, 1, 3):
        to_far(q)
    for b in range(2):
        to_next(2 + b, 1, False)
        to_next(b, -1, False)
        to_next(b, 1, True)
        to_next(2 + b, -1, True)

    def whole(q):
        return part(x, q) + r2m[q].astype(F32) + r2p[q].astype(F32)

    def across_copy(cj, b):
        return remote(zs.at[2 * cj + b], fin_z.at[b], fs.at[cj, b], fr.at[b], across[cj])

    for b in range(2):
        for q in (b, 2 + b):
            hop(1, q, r2m, xrm, 1).wait_recv()
            hop(2, q, r2p, xrp, 1).wait_recv()

        @pl.when(role == 1)
        def _():
            for cj in range(2):
                zs[2 * cj + b] = whole(2 * cj + b).astype(BF16)
                across_copy(cj, b).start()

        @pl.when(role == 0)
        def _():
            fin_s[b] = whole(2 * other + b)
            remote(fin_s.at[b], fin_f.at[b], fs.at[0, b], fd.at[b], partner).start()
            fin_f[b] = whole(2 * c + b)

    for b in range(2):
        across_copy(0, b).wait_recv()

    @pl.when(role == 1)
    def _():
        for b in range(2):
            remote(fin_s.at[b], fin_f.at[b], fs.at[0, b], fd.at[b], partner).wait_recv()

    for i in range(STAGES):
        sends_done(i)
    for n in range(12):
        remote(obuf.at[n], obuf.at[n], xs.at[n], xr1.at[0], partner).wait_send()

    @pl.when(role == 1)
    def _():
        for i in range(STAGES):
            remote(shard(i, None, given), shard(i, t_own, held), own_s.at[i], own.at[i], swap).wait_send()
        for cj in range(2):
            for b in range(2):
                across_copy(cj, b).wait_send()

    @pl.when(role == 0)
    def _():
        remote(w_in.at[1], wbuf, meta_s.at[0], meta_r.at[0], partner).wait_send()
        remote(meta_in, mbuf, meta_s.at[1], meta_r.at[1], partner).wait_send()
        for b in range(2):
            remote(fin_s.at[b], fin_f.at[b], fs.at[0, b], fd.at[b], partner).wait_send()


def per_device(env_blocks, core_blocks, mpo_coeffs, pair_left, pair_right, block_dims):
    term = lax.axis_index("term")
    sec = lax.axis_index("sec")
    ids = jnp.arange(16, dtype=jnp.int32)
    order = jnp.arange(PAIRS, dtype=jnp.int32)
    key = pair_right * PAIRS + order
    rank = jnp.sum((key[None, :] < key[:, None]).astype(jnp.int32), axis=1)
    perm = rank[None, :] == order[:, None]
    left_dim = jnp.sum(jnp.where((sec * 2 + pair_left)[:, None] == ids[None, :], block_dims[None, :], 0), axis=1)
    right_hot = pair_right[:, None] == ids[None, :]
    right_dim = jnp.sum(jnp.where(right_hot, block_dims[None, :], 0), axis=1)
    rows = term * 8 + jnp.arange(8, dtype=jnp.int32)
    cols = jnp.arange(BLK, dtype=jnp.int32)
    keep = (rows[None, :, None] < left_dim[:, None, None]) & (cols[None, None, :] < right_dim[:, None, None])
    masked = jnp.where(keep, core_blocks, jnp.zeros((), BF16))
    hot = perm.astype(BF16)
    core_sorted = jnp.einsum("kp,px->kx", hot, masked.reshape(PAIRS, 8 * BLK), preferred_element_type=F32)
    core_sorted = core_sorted.astype(BF16).reshape(PAIRS, 8, BLK)
    left_hot = (pair_left[:, None] == jnp.arange(2)[None, :]).astype(BF16)

    def weights(v):
        own = lax.dynamic_index_in_dim(mpo_coeffs, v, 1, keepdims=False)
        spread = own.T[:, :, None] * left_hot[:, None, :]
        return jnp.dot(hot, spread.reshape(PAIRS, 64), preferred_element_type=F32).astype(BF16)

    w_both = jnp.stack([weights(term), weights(term + 1 - 2 * lax.rem(term, 2))])
    counts = jnp.sum(right_hot.astype(jnp.int32), axis=0)
    ends = jnp.sum(jnp.where(ids[None, :] <= ids[:, None], counts[None, :], 0), axis=1)
    last = jnp.where(counts > 0, ends, 0)
    firsts = jnp.sum(((ends - counts)[None, :] == order[:, None]) & (counts > 0)[None, :], axis=1)
    same = (1 - firsts).astype(jnp.int32)
    meta = jnp.concatenate([same, last.astype(jnp.int32), jnp.zeros((48,), jnp.int32)]).reshape(1, 128)
    meta = jnp.broadcast_to(meta, (8, 128))
    vmem = pl.BlockSpec(memory_space=pltpu.VMEM)
    dma = pltpu.SemaphoreType.DMA
    block = (BLK, BLK)
    first, second = pl.pallas_call(
        kernel,
        name="sweep_update",
        out_shape=(jax.ShapeDtypeStruct((2, *block), F32), jax.ShapeDtypeStruct((2, *block), BF16)),
        in_specs=[vmem] * 4,
        out_specs=(vmem, vmem),
        scratch_shapes=[
            pltpu.VMEM((32, 2, *block), BF16),
            pltpu.VMEM((PAIRS, *block), BF16),
            pltpu.VMEM((PAIRS, *block), BF16),
            pltpu.VMEM((PAIRS + 1, *block), F32),
            pltpu.VMEM((8 * PAIRS, 8 * PAIRS), BF16),
            pltpu.VMEM((PAIRS, PAIRS), BF16),
            pltpu.VMEM((8, 128), jnp.int32),
            pltpu.SMEM((8, 128), jnp.int32),
            pltpu.VMEM((12, *block), BF16),
            pltpu.VMEM((4, *block), BF16),
            pltpu.VMEM((4, *block), BF16),
            pltpu.VMEM((4, *block), BF16),
            pltpu.VMEM((2, *block), F32),
            pltpu.VMEM((4, *block), BF16),
            dma((STAGES, 2, 20)),
            dma((STAGES,)),
            dma((STAGES,)),
            dma((STAGES,)),
            dma((STAGES,)),
            dma((STAGES,)),
            dma((2,)),
            dma((2,)),
            dma,
            dma((4,)),
            dma((4,)),
            dma((4,)),
            dma((12,)),
            dma((2,)),
            dma((2,)),
            dma((2, 2)),
        ],
        compiler_params=pltpu.CompilerParams(
            collective_id=0, has_side_effects=True, vmem_limit_bytes=64000 * 1024
        ),
    )(env_blocks.reshape(2, *block), core_sorted, w_both, meta)
    return (first + second.astype(F32)).reshape(1, 2, *block)


def solution(mesh):
    return jax.shard_map(
        per_device,
        mesh=mesh,
        in_specs=(
            P("term", "sec", None, None),
            P("sec", "term", None),
            P(None, None, "sec"),
            P("sec"),
            P("sec"),
            P(),
        ),
        out_specs=P("term", "sec", None, None),
        check_vma=False,
    )
```

time: 326 us -> 129 us (0.40)
  waiting for transfers between devices: 160 us -> 0 us
  Pallas kernels: 0 us -> 119 us
  blocking collectives: 56.7 us -> 0 us
  local copies, waits for them, and re-layouts: 47.3 us -> 2.38 us
  matrix products: 41.6 us -> 0.48 us
  between operations: 13.5 us -> 0.08 us
    all_gather x2 -> x0, waiting for transfers between devices: 158 us -> none  [the longest x1 101 us: per_device(): piece = lax.all_gather(env_blocks, 'term', axis=0, tiled=True)]
    pallas_call x0 -> x1, Pallas kernels: none -> 119 us  [per_device(): pl.pallas_call(kernel, name='sweep_update', out_shape=(jax.ShapeDtypeStru...]
    all_to_all x1 -> x0, blocking collectives: 56.7 us -> none  [sum_at_owner(): pieces = lax.all_to_all(split_up(array, dim, peers), axis, 0, 0, tiled=True)]
    dot_general x4 -> x3, matrix products: 41.6 us -> 0.48 us  [the longest x2 0.26 us: weights(): jnp.dot(hot, spread.reshape(PAIRS, 64), preferred_element_type=F32)]
    reshape x2 -> x0, local copies, waits for them, and re-layouts: 34.3 us -> none  [the longest x1 19.8 us: per_device(): flat = piece.reshape(count, nb_local, blk * blk)]
    unnamed x11 -> x4, local copies, waits for them, and re-layouts: 9.72 us -> 0.82 us
  transfers between devices with their start and end apart: 2 -> 0, of which waited for: 2 -> 0; matrix products, arithmetic and copies ran while one was open for 14% -> 0% of each run, Pallas kernels for 0% -> 0%
where the time goes in v1:
time: 129 us
  Pallas kernels  119 us (92%)
  other arithmetic  6.31 us (5%)
  local copies, waits for them, and re-layouts  2.38 us (2%)
    pallas_call x1, Pallas kernels, per_device(): pl.pallas_call(kernel, name='sweep_update', out_shape=(jax.ShapeDtypeStru...  119 us

profile of v1, /device:TPU:1, one launch (start us, length us, event | category | flops | bytes accessed | tf_op | source)
XLA Modules:
  0.0 128.7 jit_solution(1775634877282554488)
XLA Ops:
  0.0 0.0 copy-start
  0.0 0.7 broadcast_add_fusion
  0.7 0.7 compare_convert_fusion
  1.4 0.7 iota_add_fusion.1
  2.0 0.2 convert_reduce_fusion
  2.2 0.9 convert_reduce_fusion.2
  3.1 0.1 select_reduce_fusion
  3.2 0.1 convert_reduce_fusion.1
  3.3 0.1 pad_add_fusion
  3.4 0.6 broadcast_in_dim.44.meta_in
  4.0 0.1 broadcast_compare_fusion
  4.1 0.1 iota_compare_fusion
  4.2 1.0 constant_dynamic-slice_fusion.1
  5.2 0.1 fusion
  5.3 0.1 fusion.1
  5.4 0.6 pad_maximum_fusion.w_in
  6.1 0.0 copy-done
  6.1 0.2 and_select_fusion
  6.2 0.1 copy.13
  6.3 0.2 convolution_convert_fusion
  6.5 0.8 copy.14
  7.3 119.4 %sweep_update.1 = (f32[2,256,256]{2,1,0:T(8,128)}, bf16[2,256,256]{2,1,0:T(8,128)(2,1)}) custom-call(bf16[2,256,256]{2,1,0:T(8,128)(2,1)} %bitcast.28, bf16[64,8,256]{2,1,0:T(8,128)(2,1)} %bitcast.26, bf16[2,64,64]{2,1,0:T(8,128)(2,1)} %pad_maximum_fusion.w_in, s32[8,128]{1,0:T(8,128)} %broadcast_in_dim.44.meta_in), custom_call_target="tpu_custom_call" | custom-call | tf_op jit(solution)/shard_map/sweep_update/pallas_call | solution.py:382
  126.7 2.0 %add_bitcast_fusion = f32[1,2,256,256]{3,2,1,0:T(8,128)} fusion(f32[2,256,256]{2,1,0:T(8,128)} %get-tuple-element.7, bf16[2,256,256]{2,1,0:T(8,128)(2,1)} %get-tuple-element.8), kind=kLoop, calls=%fused_computation.5 | loop fusion | flops 262144 | bytes 1310720 | tf_op jit(solution)/shard_map/reshape | solution.py:424
  (7 shorter events, 0.1 us)
Async XLA Ops:
  0.0 6.1 %copy-start = (bf16[64,8,256]{2,1,0:T(8,128)(2,1)S(1)}, bf16[64,8,256]{2,1,0:T(8,128)(2,1)}, u32[]{:S(2)}) copy-start(bf16[64,8,256]{2,1,0:T(8,128)(2,1)} %param.7) | copy-start | bytes 786436
